TPU v7x, 32 devices: a whole 2x2x4 slice. The times are simulated.
32 devices in a mesh: line: 1, freq: 4 (over z), section: 2 (over core), rcv: 4 (over y, x).
Axes of the slice: x: 2, y: 2, z: 4, core: 2. Of those that a mesh axis runs over, the one named last changes fastest.
Arguments:
- recorded: bfloat16 [512, 512, 1024], P(('line', 'freq', 'section'), 'rcv'), may hold values from -6 to 6
- signatures: bfloat16 [512, 256], P(('line', 'freq', 'section')), may hold values from -0.375 to 0.375
- ghost_delay: int32 [512, 512], P(('line', 'freq', 'section'), 'rcv'), may hold values from 8 to 47
- dead_trace: int32 [512, 512], P(('line', 'freq', 'section'), 'rcv'), may hold values 0 or 1
Outputs:
- multiples: float32 [2, 32, 512, 512], P(None, ('freq', 'section'), 'line', 'rcv')
All inputs are finite; a program needn't handle non-finite values. No bound on the sum of `dead_trace` on one device may be relied on, other than what follows from the above.
Results may differ from a plain program's by a relative error of at most 0.0041.
Values may be sent and summed in bfloat16 or wider, within the bound.
No kernel may reach another device: no remote copies, remote signals or barrier semaphores. Data moves between devices by JAX's collectives and lax.ppermute only.
A program may use at most 320 MiB of HBM per device.

v0:
```python
import math
import jax
import jax.numpy as jnp
from jax import lax
from jax.sharding import PartitionSpec as P

BIN_DEV = 1
reflectivity = 0.6


def filter_kernel(signatures):
    shot_count, tap_count = signatures.shape
    zero_front = jnp.zeros((shot_count, tap_count), signatures.dtype)
    zero_back = jnp.zeros((shot_count, tap_count + 1), signatures.dtype)
    padded = jnp.concatenate([zero_front, signatures, zero_back], axis=1)
    width = 3 * tap_count
    rows_count = 2 * tap_count
    tiled = jnp.tile(padded, (1, rows_count))[:, : rows_count * width]
    banded = tiled.reshape(shot_count, rows_count, width)
    return banded[:, :, 2 * tap_count :]


def designature(recorded, signatures):
    shot_count, receivers, samples = recorded.shape
    tap_count = signatures.shape[1]
    blocks = samples // tap_count
    kernel = filter_kernel(signatures)
    blocked = recorded.reshape(shot_count, receivers, blocks, tap_count)
    previous_partial = jnp.concatenate(
        [jnp.zeros_like(blocked[:, :, :1]), blocked[:, :, :-1]], axis=2
    )
    window = jnp.concatenate([previous_partial, blocked], axis=3)
    filtered = jnp.einsum("srbj,sji->srbi", window, kernel, preferred_element_type=jnp.float32)
    return filtered.reshape(shot_count, receivers, samples)


def spectrum(filtered, bin_count):
    samples = filtered.shape[2]
    sample_index = jnp.arange(samples, dtype=jnp.int32)
    bin_index = jnp.arange(1, bin_count + 1, dtype=jnp.int32)
    phase_angles = (bin_index[:, None] * sample_index[None, :] % samples).astype(jnp.float32) * (
        2.0 * math.pi / samples
    )
    factor = 1.0 / math.sqrt(samples)
    twiddle = jnp.stack([jnp.cos(phase_angles) * factor, -jnp.sin(phase_angles) * factor])
    return jnp.einsum("srt,pft->pfsr", filtered, twiddle, precision=lax.Precision.HIGHEST)


def deghost(spectra, ghost_delay, dead_trace, samples):
    bin_count = spectra.shape[1]
    bin_index = jnp.arange(1, bin_count + 1, dtype=jnp.int32)
    phase_angles = (bin_index[:, None, None] * ghost_delay[None] % samples).astype(jnp.float32) * (
        2.0 * math.pi / samples
    )
    cosine = jnp.cos(phase_angles)
    sine_value = jnp.sin(phase_angles)
    divisor = 1.0 - 2.0 * reflectivity * cosine + reflectivity * reflectivity
    gain_real = (1.0 - reflectivity * cosine) / divisor
    gain_imag = -reflectivity * sine_value / divisor
    live_mask = (1 - dead_trace).astype(jnp.float32)[None]
    real_part = (spectra[0] * gain_real - spectra[1] * gain_imag) * live_mask
    imag_part = (spectra[0] * gain_imag + spectra[1] * gain_real) * live_mask
    return jnp.stack([real_part, imag_part]).astype(jnp.bfloat16)


def multiply(left_operand, right_operand):
    return jnp.einsum(
        "uxy,uym->uxm", left_operand, right_operand, preferred_element_type=jnp.float32
    )


def complex_product(left_operand, right_operand):
    real_out = multiply(left_operand[0], right_operand[0]) - multiply(
        left_operand[1], right_operand[1]
    )
    imag_out = multiply(left_operand[0], right_operand[1]) + multiply(
        left_operand[1], right_operand[0]
    )
    return jnp.stack([real_out, imag_out])


def per_device(recorded, signatures, ghost_delay, dead_trace):
    samples = recorded.shape[2]
    bin_count = BIN_DEV * lax.axis_size("freq") * lax.axis_size("section") * lax.axis_size("rcv")
    filtered = designature(recorded, signatures)
    spectra = spectrum(filtered, bin_count)
    deghosted = deghost(spectra, ghost_delay, dead_trace, samples)
    relayed = lax.all_to_all(
        deghosted, ("freq", "section"), split_axis=1, concat_axis=2, tiled=True
    )
    summed = complex_product(lax.all_gather(relayed, "rcv", axis=3, tiled=True), relayed)
    station_count = relayed.shape[2]
    return summed * (1.0 / math.sqrt(station_count))


def solution(mesh):
    return jax.shard_map(
        per_device,
        mesh=mesh,
        in_specs=(
            P(("line", "freq", "section"), "rcv", None),
            P(("line", "freq", "section"), None),
            P(("line", "freq", "section"), "rcv"),
            P(("line", "freq", "section"), "rcv"),
        ),
        out_specs=P(None, ("freq", "section"), "line", "rcv"),
        check_vma=False,
    )
```

profile of v0, /device:TPU:0, one launch (start us, length us, event | category | flops | bytes accessed | tf_op | source)
XLA Modules:
  0.0 433.4 jit_solution(421783146112873044)
XLA Ops:
  6.5 0.0 all-gather.2.cloned.1.call-start
  6.5 22.3 %copy.16 = bf16[64,128,1024]{1,2,0:T(8,128)(2,1)} copy(bf16[64,128,1024]{2,1,0:T(8,128)(2,1)} %param.4) | data formatting | bytes 33554432 | tf_op args[0]
  28.8 22.4 %copy.17 = bf16[64,128,4,256]{3,1,2,0:T(8,128)(2,1)} copy(bf16[64,128,4,256]{1,3,2,0:T(8,128)(2,1)} %bitcast.49) | data formatting | bytes 33554432 | tf_op jit(solution)/shard_map/reshape | solution.py:28
  51.2 0.0 copy-start.1
  51.2 10.7 %slice.44 = bf16[64,128,3,256]{3,1,2,0:T(8,128)(2,1)} slice(bf16[64,128,4,256]{3,1,2,0:T(8,128)(2,1)} %copy.17), slice={[0:64], [0:128], [0:3], [0:256]} | slice | bytes 25165824 | tf_op jit(solution)/shard_map/slice | solution.py:30
  62.0 0.0 copy-done.1
  62.0 18.8 %tile.4 = bf16[64,512,769]{2,1,0:T(8,128)(2,1)} broadcast(bf16[64,769]{1,0:T(8,128)(2,1)S(1)} %maximum_maximum_fusion), dimensions={0,2} | broadcast | bytes 50495616 | tf_op jit(solution)/shard_map/tile | solution.py:18
  80.9 122.3 %tile.10 = bf16[64,393728]{1,0:T(8,128)(2,1)} reshape(bf16[64,512,769]{2,1,0:T(8,128)(2,1)} %tile.4) | data formatting | bytes 100794368 | tf_op jit(solution)/shard_map/tile | solution.py:18
  203.2 33.3 %slice.45 = bf16[64,393216]{1,0:T(8,128)(2,1)} slice(bf16[64,393728]{1,0:T(8,128)(2,1)} %tile.10), slice={[0:64], [0:393216]} | slice | bytes 100663296 | tf_op jit(solution)/shard_map/slice | solution.py:18
  236.5 0.0 copy-start.2
  236.5 34.2 %copy.28 = bf16[8,8,512,768]{3,2,1,0:T(8,128)(2,1)} copy(bf16[8,8,512,768]{3,1,2,0:T(8,128)(2,1)} %bitcast.48) | data formatting | bytes 100663296
  270.7 0.6 cosine_multiply_fusion
  271.3 0.0 copy-done.2
  271.3 29.4 %fusion.2 = f32[64,128,4,256]{1,3,2,0:T(8,128)} fusion(bf16[64,128,3,256]{3,1,2,0:T(8,128)(2,1)} %slice.44, bf16[64,128,4,256]{3,1,2,0:T(8,128)(2,1)} %copy.17, bf16[64,512,768]{2,1,0:T(8,128)(2,1)} %bitcast.50), kind=kOutput, calls=%fused_computation.3 | convolution fusion | flops 8690597888 | bytes 79691776 | tf_op jit(solution)/shard_map/srbj,sji->srbi/dot_general | solution.py:33
  300.7 0.0 copy-start
  300.7 24.1 %fusion.20 = f32[2,32,64,128]{3,1,2,0:T(8,128)S(1)} fusion(f32[64,128,1024,1]{1,2,0,3:T(8,128)} %bitcast.51, f32[1,32,1024]{2,1,0:T(8,128)S(1)} %get-tuple-element.12, f32[1,32,1024]{2,1,0:T(8,128)S(1)} %get-tuple-element.11), kind=kOutput, calls=%fused_computation.36 | convolution fusion | flops 6442516480 | bytes 35913728 | tf_op jit(solution)/shard_map/srt,pft->pfsr/dot_general | solution.py:46
  324.8 0.0 copy-done
  324.8 5.1 %multiply_convert_fusion.1 = (bf16[1,32,64,128]{3,1,2,0:T(8,128)(2,1)S(1)}, bf16[1,32,64,128]{3,1,2,0:T(8,128)(2,1)S(1)}) fusion(f32[2,32,64,128]{3,1,2,0:T(8,128)S(1)} %fusion.20, f32[64,128]{1,0:T(8,128)S(1)} %subtract_convert_fusion, s32[64,128]{1,0:T(8,128)S(1)} %copy-done, s32[32]{0:T(128)S(1)} %iota_add_fusion), kind=kLoop, calls=%fused_computation.30 | loop fusion | flops 8126464 | bytes 3211392 | tf_op jit(solution)/shard_map/convert
  329.9 0.1 pad_maximum_fusion
  330.0 0.4 copy.21
  330.4 32.7 %all_to_all.18 = bf16[2,32,64,128]{3,2,0,1:T(8,128)(2,1)S(1)} all-to-all(bf16[2,32,64,128]{3,2,0,1:T(8,128)(2,1)S(1)} %copy.21), channel_id=1, replica_groups=mesh['line'=1,'freq'=4,'section'=2,'rcv'=4] {'freq','section'}, dimensions={1} | all-to-all | bytes 2097152 | tf_op jit(solution)/shard_map/all_to_all | solution.py:88
  363.1 1.1 copy.31
  364.2 0.0 all-gather.2.cloned.1.call-update
  364.2 1.3 fusion.33
  365.5 50.3 %all-gather.2.cloned.1.call-done = bf16[2,4,512,512]{3,2,1,0:T(8,128)(2,1)} async-done(((bf16[2,4,512,128]{3,2,1,0:T(8,128)(2,1)}), bf16[2,4,512,512]{3,2,1,0:T(8,128)(2,1)}) %all-gather.2.cloned.1.call-update) | async-done | bytes 4194320 | tf_op jit(solution)/shard_map/all_gather | solution.py:91
  415.8 2.3 fusion.9
  418.1 2.3 fusion.8
  420.4 2.3 fusion.13
  422.8 2.3 fusion.15
  425.1 1.5 maximum_multiply_fusion
  (7 shorter events, 0.1 us)
Async XLA Ops:
  6.5 409.3 %all-gather.2.cloned.1.call-start = ((), (), s32[]{:S(2)}) async-start(), calls=%async_computation.1 | async-start | bytes 5242880 | tf_op jit(solution)/shard_map/all_gather | solution.py:91
  51.2 10.8 %copy-start.1 = (bf16[64,256]{1,0:T(8,128)(2,1)S(1)}, bf16[64,256]{1,0:T(8,128)(2,1)}, u32[]{:S(2)}) copy-start(bf16[64,256]{1,0:T(8,128)(2,1)} %param.5) | copy-start | bytes 98308
  236.5 34.8 %copy-start.2 = (s32[64,128]{1,0:T(8,128)S(1)}, s32[64,128]{1,0:T(8,128)}, u32[]{:S(2)}) copy-start(s32[64,128]{1,0:T(8,128)} %param.7) | copy-start | bytes 98308
  300.7 24.1 %copy-start = (s32[64,128]{1,0:T(8,128)S(1)}, s32[64,128]{1,0:T(8,128)}, u32[]{:S(2)}) copy-start(s32[64,128]{1,0:T(8,128)} %param.6) | copy-start | bytes 98308
Sparse Core Ops, SparseCore 0:
  364.3 51.4 all-gather.1
where the time goes:
time: 435 us; the launch traced here: 433 us
  local copies, waits for them, and re-layouts  267 us (61%)
  matrix products  62.7 us (14%)
  waiting for transfers between devices  50.3 us (12%)
  blocking collectives  32.7 us (8%)
  between operations  13.5 us (3%)
  other arithmetic  7.29 us (2%)
    another operation x2, local copies, waits for them, and re-layouts, filter_kernel(): tiled = jnp.tile(padded, (1, rows_count))[:, :rows_count * width]  141 us
    unnamed x8, local copies, waits for them, and re-layouts  56.5 us
    all_gather x1, waiting for transfers between devices, per_device(): lax.all_gather(relayed, 'rcv', axis=3, tiled=True)  50.3 us
    slice x1, local copies, waits for them, and re-layouts, filter_kernel(): tiled = jnp.tile(padded, (1, rows_count))[:, :rows_count * width]  33.3 us
    all_to_all x1, blocking collectives, per_device(): lax.all_to_all(deghosted, ('freq', 'section'), split_axis=1, concat_axis=...  32.7 us
    dot_general x1, matrix products, designature(): jnp.einsum('srbj,sji->srbi', window, kernel, preferred_element_type=jnp.f...  29.4 us
    dot_general x1, matrix products, spectrum(): jnp.einsum('srt,pft->pfsr', filtered, twiddle, precision=lax.Precision.HI...  24.1 us
    reshape x1, local copies, waits for them, and re-layouts, designature(): blocked = recorded.reshape(shot_count, receivers, blocks, tap_count)  22.4 us
  transfers between devices with their start and end apart: 1, of which 1 were waited for; matrix products, arithmetic and copies ran while one was open for 0% of the time, Pallas kernels for 0%

commit v1 on v0

--- a/solution.py
+++ b/solution.py
@@ -6,6 +6,22 @@
 
 BIN_DEV = 1
 reflectivity = 0.6
+
+
+def swapped_with_each(value, axis, split, join):
+    ways, here = (lax.axis_size(axis), lax.axis_index(axis))
+    width = value.shape[split] // ways
+    lengths = list(value.shape)
+    lengths[split] = width
+    height = lengths[join]
+    lengths[join] = height * ways
+    full = jnp.zeros(lengths, value.dtype)
+    for mask in range(ways):
+        part = lax.dynamic_slice_in_dim(value, (here ^ mask) * width, width, axis=split)
+        if mask:
+            part = lax.ppermute(part, axis, [(d, d ^ mask) for d in range(ways)])
+        full = lax.dynamic_update_slice_in_dim(full, part, (here ^ mask) * height, axis=join)
+    return full
 
 
 def filter_kernel(signatures):
@@ -85,9 +101,7 @@
     filtered = designature(recorded, signatures)
     spectra = spectrum(filtered, bin_count)
     deghosted = deghost(spectra, ghost_delay, dead_trace, samples)
-    relayed = lax.all_to_all(
-        deghosted, ("freq", "section"), split_axis=1, concat_axis=2, tiled=True
-    )
+    relayed = swapped_with_each(deghosted, ("freq", "section"), 1, 2)
     summed = complex_product(lax.all_gather(relayed, "rcv", axis=3, tiled=True), relayed)
     station_count = relayed.shape[2]
     return summed * (1.0 / math.sqrt(station_count))

time: 435 us -> 434 us (level)
  blocking collectives: 32.7 us -> 0 us
  waiting for transfers between devices: 50.3 us -> 72 us
  starting transfers between devices: 0.01 us -> 9.52 us
    all_to_all x1 -> x0, blocking collectives: 32.7 us -> none  [per_device(): lax.all_to_all(deghosted, ('freq', 'section'), split_axis=1, concat_axis=...]
    ppermute x0 -> x7, waiting for transfers between devices: none -> 13.8 us  [swapped_with_each(): part = lax.ppermute(part, axis, [(d, d ^ mask) for d in range(ways)])]
    ppermute x0 -> x7, starting transfers between devices: none -> 9.52 us  [swapped_with_each(): part = lax.ppermute(part, axis, [(d, d ^ mask) for d in range(ways)])]
    all_gather x1, waiting for transfers between devices: 50.3 us -> 58.2 us  [per_device(): lax.all_gather(relayed, 'rcv', axis=3, tiled=True)]
    unnamed x8 -> x10, local copies, waits for them, and re-layouts: 56.5 us -> 57.4 us
  transfers between devices with their start and end apart: 1 -> 8, of which waited for: 1 -> 4; matrix products, arithmetic and copies ran while one was open for 0% -> 0% of each run, Pallas kernels for 0% -> 0%
where the time goes in v1:
time: 434 us; the launch traced here: 432 us
  local copies, waits for them, and re-layouts  265 us (61%)
  waiting for transfers between devices  72 us (17%)
  matrix products  63 us (15%)
  between operations  13.6 us (3%)
  starting transfers between devices  9.52 us (2%)
  other arithmetic  8.52 us (2%)
    another operation x2, local copies, waits for them, and re-layouts, filter_kernel(): tiled = jnp.tile(padded, (1, rows_count))[:, :rows_count * width]  141 us
    all_gather x1, waiting for transfers between devices, per_device(): lax.all_gather(relayed, 'rcv', axis=3, tiled=True)  58.2 us
    unnamed x10, local copies, waits for them, and re-layouts  57.4 us
    slice x1, local copies, waits for them, and re-layouts, filter_kernel(): tiled = jnp.tile(padded, (1, rows_count))[:, :rows_count * width]  33.3 us
    dot_general x1, matrix products, designature(): jnp.einsum('srbj,sji->srbi', window, kernel, preferred_element_type=jnp.f...  29.4 us
    dot_general x1, matrix products, spectrum(): jnp.einsum('srt,pft->pfsr', filtered, twiddle, precision=lax.Precision.HI...  24.1 us
    reshape x1, local copies, waits for them, and re-layouts, designature(): blocked = recorded.reshape(shot_count, receivers, blocks, tap_count)  22.4 us
    ppermute x7, waiting for transfers between devices, swapped_with_each(): part = lax.ppermute(part, axis, [(d, d ^ mask) for d in range(ways)])  13.8 us
  transfers between devices with their start and end apart: 8, of which 4 were waited for; matrix products, arithmetic and copies ran while one was open for 0% of the time, Pallas kernels for 0%

profile of v1, /device:TPU:0, one launch (start us, length us, event | category | flops | bytes accessed | tf_op | source)
XLA Modules:
  0.0 432.1 jit_solution(8157966442795181447)
XLA Ops:
  6.5 0.0 all-gather.2.cloned.1.call-start
  6.5 22.3 %copy.13 = bf16[64,128,1024]{1,2,0:T(8,128)(2,1)} copy(bf16[64,128,1024]{2,1,0:T(8,128)(2,1)} %param.4) | data formatting | bytes 33554432 | tf_op args[0]
  28.8 22.4 %copy.14 = bf16[64,128,4,256]{3,1,2,0:T(8,128)(2,1)} copy(bf16[64,128,4,256]{1,3,2,0:T(8,128)(2,1)} %bitcast.46) | data formatting | bytes 33554432 | tf_op jit(solution)/shard_map/reshape | solution.py:44
  51.2 0.0 copy-start.2
  51.2 10.6 %slice.42 = bf16[64,128,3,256]{3,1,2,0:T(8,128)(2,1)} slice(bf16[64,128,4,256]{3,1,2,0:T(8,128)(2,1)} %copy.14), slice={[0:64], [0:128], [0:3], [0:256]} | slice | bytes 25165824 | tf_op jit(solution)/shard_map/slice | solution.py:46
  61.9 0.0 copy-done.2
  61.9 18.8 %tile.4 = bf16[64,512,769]{2,1,0:T(8,128)(2,1)} broadcast(bf16[64,769]{1,0:T(8,128)(2,1)S(1)} %maximum_maximum_fusion), dimensions={0,2} | broadcast | bytes 50495616 | tf_op jit(solution)/shard_map/tile | solution.py:34
  80.7 122.4 %tile.10 = bf16[64,393728]{1,0:T(8,128)(2,1)} reshape(bf16[64,512,769]{2,1,0:T(8,128)(2,1)} %tile.4) | data formatting | bytes 100794368 | tf_op jit(solution)/shard_map/tile | solution.py:34
  203.0 33.3 %slice.43 = bf16[64,393216]{1,0:T(8,128)(2,1)} slice(bf16[64,393728]{1,0:T(8,128)(2,1)} %tile.10), slice={[0:64], [0:393216]} | slice | bytes 100663296 | tf_op jit(solution)/shard_map/slice | solution.py:34
  236.4 0.0 copy-start.3
  236.4 34.2 %copy.31 = bf16[8,8,512,768]{3,2,1,0:T(8,128)(2,1)} copy(bf16[8,8,512,768]{3,1,2,0:T(8,128)(2,1)} %bitcast.45) | data formatting | bytes 100663296
  270.5 0.6 cosine_multiply_fusion
  271.1 0.0 copy-done.3
  271.2 29.4 %fusion.2 = f32[64,128,4,256]{1,3,2,0:T(8,128)} fusion(bf16[64,128,3,256]{3,1,2,0:T(8,128)(2,1)} %slice.42, bf16[64,128,4,256]{3,1,2,0:T(8,128)(2,1)} %copy.14, bf16[64,512,768]{2,1,0:T(8,128)(2,1)} %bitcast.47), kind=kOutput, calls=%fused_computation.3 | convolution fusion | flops 8690597888 | bytes 79691776 | tf_op jit(solution)/shard_map/srbj,sji->srbi/dot_general | solution.py:49
  300.6 0.0 copy-start.1
  300.6 24.1 %fusion.20 = f32[2,32,64,128]{3,1,2,0:T(8,128)S(1)} fusion(f32[64,128,1024,1]{1,2,0,3:T(8,128)} %bitcast.48, f32[1,32,1024]{2,1,0:T(8,128)S(1)} %get-tuple-element.16, f32[1,32,1024]{2,1,0:T(8,128)S(1)} %get-tuple-element.15), kind=kOutput, calls=%fused_computation.53 | convolution fusion | flops 6442516480 | bytes 35913728 | tf_op jit(solution)/shard_map/srt,pft->pfsr/dot_general | solution.py:62
  324.7 0.0 copy-done.1
  324.7 5.1 %multiply_convert_fusion = (bf16[1,32,64,128]{3,1,2,0:T(8,128)(2,1)S(1)}, bf16[1,32,64,128]{3,1,2,0:T(8,128)(2,1)S(1)}) fusion(f32[2,32,64,128]{3,1,2,0:T(8,128)S(1)} %fusion.20, f32[64,128]{1,0:T(8,128)S(1)} %subtract_convert_fusion, s32[64,128]{1,0:T(8,128)S(1)} %copy-done.1, s32[32]{0:T(128)S(1)} %iota_add_fusion), kind=kLoop, calls=%fused_computation.44 | loop fusion | flops 8126464 | bytes 3211392 | tf_op jit(solution)/shard_map/convert.1
  329.8 1.2 fusion.23
  331.0 0.5 collective-permute-start
  331.4 2.6 collective-permute-start.1
  334.0 0.1 collective-permute-start.2
  334.1 2.7 collective-permute-start.3
  336.9 0.1 fusion.30
  337.0 0.1 collective-permute-start.4
  337.1 0.1 broadcast_in_dim.6
  337.3 0.0 collective-permute-done
  337.3 3.5 collective-permute-start.5
  340.9 2.8 collective-permute-done.1
  343.8 0.0 collective-permute-start.6
  343.8 2.5 collective-permute-done.2
  346.3 0.0 collective-permute-done.3
  346.4 8.4 %collective-permute-done.4 = bf16[2,4,64,128]{3,1,2,0:T(4,128)(2,1)S(1)} collective-permute-done((bf16[2,4,64,128]{3,1,2,0:T(4,128)(2,1)S(1)}, bf16[2,4,64,128]{3,1,2,0:T(4,128)(2,1)S(1)}, u32[]{:S(2)}, u32[]{:S(2)}) %collective-permute-start.4) | collective-permute-done | bytes 131104 | tf_op jit(solution)/shard_map/ppermute | solution.py:22
  354.8 0.0 collective-permute-done.5
  354.9 0.0 collective-permute-done.6
  355.0 0.0 copy-start
  355.0 1.0 copy-done
  355.9 0.0 all-gather.2.cloned.1.call-update
  356.0 58.2 %all-gather.2.cloned.1.call-done = bf16[2,4,512,512]{3,2,1,0:T(8,128)(2,1)} async-done(((bf16[2,4,512,128]{3,2,1,0:T(8,128)(2,1)}), bf16[2,4,512,512]{3,2,1,0:T(8,128)(2,1)}) %all-gather.2.cloned.1.call-update) | async-done | bytes 4194320 | tf_op jit(solution)/shard_map/all_gather | solution.py:105
  414.1 2.4 fusion.11
  416.5 2.4 fusion.10
  418.9 2.4 fusion.13
  421.3 2.4 fusion.15
  423.7 1.5 maximum_multiply_fusion
  (15 shorter events, 0.4 us)
Async XLA Ops:
  6.5 407.6 %all-gather.2.cloned.1.call-start = ((), (), s32[]{:S(2)}) async-start(), calls=%async_computation | async-start | bytes 5242880 | tf_op jit(solution)/shard_map/all_gather | solution.py:105
  51.2 10.7 %copy-start.2 = (bf16[64,256]{1,0:T(8,128)(2,1)S(1)}, bf16[64,256]{1,0:T(8,128)(2,1)}, u32[]{:S(2)}) copy-start(bf16[64,256]{1,0:T(8,128)(2,1)} %param.5) | copy-start | bytes 98308
  236.4 34.8 %copy-start.3 = (s32[64,128]{1,0:T(8,128)S(1)}, s32[64,128]{1,0:T(8,128)}, u32[]{:S(2)}) copy-start(s32[64,128]{1,0:T(8,128)} %param.7) | copy-start | bytes 98308
  300.6 24.1 %copy-start.1 = (s32[64,128]{1,0:T(8,128)S(1)}, s32[64,128]{1,0:T(8,128)}, u32[]{:S(2)}) copy-start(s32[64,128]{1,0:T(8,128)} %param.6) | copy-start | bytes 98308
  331.0 6.4 %collective-permute-start = (bf16[2,4,64,128]{3,1,2,0:T(4,128)(2,1)}, bf16[2,4,64,128]{3,1,2,0:T(4,128)(2,1)S(1)}, u32[]{:S(2)}, u32[]{:S(2)}) collective-permute-start(bf16[2,4,64,128]{3,1,2,0:T(4,128)(2,1)} %get-tuple-element.9), channel_id=1, source_target_pairs={{0,4},{4,0},{8,12},{12,8},{16,20},{20,16},{24,28},{28,24},{1,5},{5... | collective-permute-start | bytes 393224 | tf_op jit(solution)/shard_map/ppermute | solution.py:22
  331.4 12.3 %collective-permute-start.1 = (bf16[2,4,64,128]{3,1,2,0:T(4,128)(2,1)}, bf16[2,4,64,128]{3,1,2,0:T(4,128)(2,1)S(1)}, u32[]{:S(2)}, u32[]{:S(2)}) collective-permute-start(bf16[2,4,64,128]{3,1,2,0:T(4,128)(2,1)} %get-tuple-element.10), channel_id=1, source_target_pairs={{0,8},{4,12},{8,0},{12,4},{16,24},{20,28},{24,16},{28,20},{1,9},{5... | collective-permute-start | bytes 393224 | tf_op jit(solution)/shard_map/ppermute | solution.py:22
  334.0 12.3 %collective-permute-start.2 = (bf16[2,4,64,128]{3,1,2,0:T(4,128)(2,1)S(1)}, bf16[2,4,64,128]{3,1,2,0:T(4,128)(2,1)S(1)}, u32[]{:S(2)}, u32[]{:S(2)}) collective-permute-start(bf16[2,4,64,128]{3,1,2,0:T(4,128)(2,1)S(1)} %get-tuple-element.11), channel_id=1, source_target_pairs={{0,12},{4,8},{8,4},{12,0},{16,28},{20,24},{24,20},{28,16},{1,13},{... | collective-permute-start | bytes 393224 | tf_op jit(solution)/shard_map/ppermute | solution.py:22
  334.1 12.2 %collective-permute-start.3 = (bf16[2,4,64,128]{3,1,2,0:T(4,128)(2,1)S(1)}, bf16[2,4,64,128]{3,1,2,0:T(4,128)(2,1)S(1)}, u32[]{:S(2)}, u32[]{:S(2)}) collective-permute-start(bf16[2,4,64,128]{3,1,2,0:T(4,128)(2,1)S(1)} %get-tuple-element.12), channel_id=1, source_target_pairs={{0,16},{4,20},{8,24},{12,28},{16,0},{20,4},{24,8},{28,12},{1,17},{... | collective-permute-start | bytes 393224 | tf_op jit(solution)/shard_map/ppermute | solution.py:22
  337.0 17.8 %collective-permute-start.4 = (bf16[2,4,64,128]{3,1,2,0:T(4,128)(2,1)S(1)}, bf16[2,4,64,128]{3,1,2,0:T(4,128)(2,1)S(1)}, u32[]{:S(2)}, u32[]{:S(2)}) collective-permute-start(bf16[2,4,64,128]{3,1,2,0:T(4,128)(2,1)S(1)} %get-tuple-element.14), channel_id=1, source_target_pairs={{0,20},{4,16},{8,28},{12,24},{16,4},{20,0},{24,12},{28,8},{1,21},{... | collective-permute-start | bytes 393224 | tf_op jit(solution)/shard_map/ppermute | solution.py:22
  337.3 17.5 %collective-permute-start.5 = (bf16[2,4,64,128]{3,1,2,0:T(4,128)(2,1)S(1)}, bf16[2,4,64,128]{3,1,2,0:T(4,128)(2,1)S(1)}, u32[]{:S(2)}, u32[]{:S(2)}) collective-permute-start(bf16[2,4,64,128]{3,1,2,0:T(4,128)(2,1)S(1)} %get-tuple-element.13), channel_id=1, source_target_pairs={{0,24},{4,28},{8,16},{12,20},{16,8},{20,12},{24,0},{28,4},{1,25},{... | collective-permute-start | bytes 393224 | tf_op jit(solution)/shard_map/ppermute | solution.py:22
  343.8 11.1 %collective-permute-start.6 = (bf16[2,4,64,128]{3,1,2,0:T(4,128)(2,1)S(1)}, bf16[2,4,64,128]{3,1,2,0:T(4,128)(2,1)S(1)}, u32[]{:S(2)}, u32[]{:S(2)}) collective-permute-start(bf16[2,4,64,128]{3,1,2,0:T(4,128)(2,1)S(1)} %get-tuple-element.7), channel_id=1, source_target_pairs={{0,28},{4,24},{8,20},{12,16},{16,12},{20,8},{24,4},{28,0},{1,29},{... | collective-permute-start | bytes 393224 | tf_op jit(solution)/shard_map/ppermute | solution.py:22
  355.0 1.0 copy-start
Sparse Core Ops, SparseCore 0:
  356.1 58.0 all-gather.1
